TPU v7x, 256 devices: a whole 4x4x8 slice. The times are simulated.
256 devices in a mesh: dom: 32 (over y_hi, z, core), col: 8 (over x, y_lo).
Axes of the slice: x: 4, y: 4 (y_hi: 2, y_lo: 2; y = y_hi * 2 + y_lo), z: 8, core: 2. Of those that a mesh axis runs over, the one named last changes fastest.
Arguments:
- tmat: bfloat16 [131072, 4096], P('dom', 'col'), may hold values from -6 to 6
- stored_mass_blocks: bfloat16 [8192, 128, 128], P('dom'), may hold values from -0.0007324219 to 0.0007324219
- block_index: int32 [8192, 2], P('dom'), may hold values from 0 to 35, as said below
- live_block_count: int32 [32], P('dom'), may hold values from 36 to 256, as said below
- send_rows: int32 [64, 256], P('dom'), may hold values from 0 to 4095, as said below
Outputs:
- reduced: float32 [512, 4096], P('dom', 'col')
Inputs may be any that keep to these rules, and one draw needn't show every extreme that they name: `block_index`: row entries lie in 0 to 31 and column entries in 0 to 35. In each partition's list slot k < 32 is block (k, k), and slot 32 + m for m < 4 has block column 32 + m. `live_block_count`: some partition uses all 256 slots in every draw. `send_rows`: the 256 rows in each list are distinct local row numbers of the sending partition.
All inputs are finite; a program needn't handle non-finite values.
Results may differ from a plain program's by a relative error of at most 0.0029.
Values may be sent and summed in bfloat16 or wider, within the bound.
A program may use at most 128 MiB of HBM per device.

v0:
```python
import jax
import jax.numpy as jnp
from jax import lax
from jax.sharding import PartitionSpec as P


def passed_along(block, axis, distance):
    devices = range(lax.axis_size(axis))
    route = [(i - distance, i) for i in devices if i - distance in devices]
    return lax.ppermute(block, axis, route)


def broadcast(block, axis, holder):
    block = jnp.where(lax.axis_index(axis) == holder, block, jnp.zeros_like(block))
    return lax.psum(block, axis)


def contract(left, right):
    return lax.dot_general(
        left, right, (((0,), (0,)), ((), ())), preferred_element_type=jnp.float32
    )


def mass_product(panel, stored_mass_blocks, block_index, live_block_count, send_rows):
    rows_dev, width = panel.shape
    bsize = stored_mass_blocks.shape[1]
    nrows_blk = rows_dev // bsize
    slot_number = stored_mass_blocks.shape[0]
    to_lower = jnp.take(panel, send_rows[0], axis=0)
    to_upper = jnp.take(panel, send_rows[1], axis=0)
    from_lower = passed_along(to_upper, "dom", 1)
    from_upper = passed_along(to_lower, "dom", -1)
    extended = jnp.concatenate([panel, from_lower, from_upper], 0).reshape(-1, bsize, width)
    live_flags = (jnp.arange(slot_number) < live_block_count[0]).astype(jnp.float32)
    partition_groups = 4
    partition_group_width = slot_number // partition_groups

    def step(acc, group):
        begin = group * partition_group_width
        blocks = lax.dynamic_slice_in_dim(stored_mass_blocks, begin, partition_group_width, 0)
        columns = lax.dynamic_slice_in_dim(block_index[:, 1], begin, partition_group_width, 0)
        targets = lax.dynamic_slice_in_dim(block_index[:, 0], begin, partition_group_width, 0)
        weights = lax.dynamic_slice_in_dim(live_flags, begin, partition_group_width, 0)
        selected = jnp.take(extended, columns, axis=0)
        prod = jnp.einsum("kab,kbw->kaw", blocks, selected, preferred_element_type=jnp.float32)
        acc = acc.at[targets].add(prod * weights[:, None, None])
        return (acc, None)

    start_acc = jnp.zeros((nrows_blk, bsize, width), jnp.float32)
    summed, _ = lax.scan(step, start_acc, jnp.arange(partition_groups))
    return summed.reshape(rows_dev, width).astype(jnp.bfloat16)


def body(tmat, stored_mass_blocks, block_index, live_block_count, send_rows):
    n_col = lax.axis_size("col")
    n_dom = lax.axis_size("dom")
    panel_width = tmat.shape[1]
    panel = broadcast(tmat, "col", n_col - 1)
    interface_mass_panel = mass_product(
        panel, stored_mass_blocks, block_index, live_block_count, send_rows
    )
    share = panel_width // n_dom
    total = lax.psum(contract(interface_mass_panel, tmat), "dom")
    return lax.dynamic_slice_in_dim(total, lax.axis_index("dom") * share, share, 0)


def solution(mesh):
    return jax.shard_map(
        body,
        mesh=mesh,
        in_specs=(P("dom", "col"), P("dom", None, None), P("dom", None), P("dom"), P("dom", None)),
        out_specs=P("dom", "col"),
        check_vma=False,
    )
```

profile of v0, /device:TPU:1, one launch (start us, length us, event | category | flops | bytes accessed | tf_op | source)
XLA Modules:
  0.0 749.2 jit_solution(13269119770228952049)
XLA Ops:
  6.5 2.2 broadcast_select_fusion
  9.0 192.5 %all-reduce.3.cloned.1.call-done = bf16[4096,512]{1,0:T(8,128)(2,1)} async-done(((bf16[4096,512]{1,0:T(8,128)(2,1)}), bf16[4096,512]{1,0:T(8,128)(2,1)}) %all-reduce.3.cloned.1.call-update) | async-done | bytes 4194320 | tf_op jit(solution)/shard_map/psum | solution.py:15
  201.5 3.9 gather_fusion.1
  205.5 3.7 collective-permute-start
  209.3 3.9 gather_fusion.2
  216.0 5.1 collective-permute-done.1
  221.0 4.0 pad_maximum_fusion
  225.0 4.3 broadcast_in_dim.27
  229.3 233.0 %while.10 = (s32[]{:T(128)}, f32[32,128,512]{2,1,0:T(8,128)}, s32[256,2]{0,1:T(2,128)S(1)}, s32[4]{0:T(128)S(1)}, bf16[256,128,128]{2,1,0:T(8,128)(2,1)}, /*inde...) while((s32[]{:T(128)}, f32[32,128,512]{2,1,0:T(8,128)}, ...), condition=%wide.region_3.5_spmd, body=%wide.region_1.0_spmd.sunk | while | flops 1086326400 | bytes 94382912 | solution.py:50
  230.9 7.9 %gather_fusion = bf16[64,128,512]{2,1,0:T(8,128)(2,1)} fusion(bf16[36,128,512]{2,1,0:T(8,128)(2,1)} %get-tuple-element.142, s32[1024]{0:T(1024)S(1)} %pad_clamp_fusion.4), kind=kCustom, calls=%fused_computation.1.clone.1 | custom fusion | bytes 16777472 | tf_op jit(solution)/shard_map/while/body/eval_jaxpr/jit(_take)/gather | solution.py:44
  238.8 12.2 %convolution_multiply_fusion.2 = f32[64,128,512]{2,1,0:T(8,128)} fusion(f32[64]{0:T(128)S(1)} %dynamic_slice.39, bf16[64,128,512]{2,1,0:T(8,128)(2,1)} %gather_fusion, pred[64]{0:T(512)(128)(4,1)S(1)} %get-tuple-element.114, bf16[256,128,128]{2,1,0:T(8,128)(2,1)} %get-tuple-element.141, s32[]{:T(128)S(6)} %select_n.70), kind=kOutput, calls=%fused_computation.4.clone.1 | convolution fusion | flops 1082130432 | bytes 27263300 | tf_op jit(solution)/shard_map/while/body/eval_jaxpr/kab,kbw->kaw/dot_general | solution.py:45
  251.0 36.9 %scatter_fusion = f32[32,128,512]{2,1,0:T(8,128)} fusion(f32[32,128,512]{2,1,0:T(8,128)} %get-tuple-element.127, s32[64]{0:T(128)S(1)} %fusion.19, f32[64,128,512]{2,1,0:T(8,128)} %convolution_multiply_fusion.2), kind=kCustom, calls=%fused_computation.3.clone.1 | custom fusion | flops 4194304 | bytes 50331904 | tf_op jit(solution)/shard_map/while/body/eval_jaxpr/scatter-add | solution.py:46
  289.5 7.9 %gather_fusion = bf16[64,128,512]{2,1,0:T(8,128)(2,1)} fusion(bf16[36,128,512]{2,1,0:T(8,128)(2,1)} %get-tuple-element.142, s32[1024]{0:T(1024)S(1)} %pad_clamp_fusion.4), kind=kCustom, calls=%fused_computation.1.clone.1 | custom fusion | bytes 16777472 | tf_op jit(solution)/shard_map/while/body/eval_jaxpr/jit(_take)/gather | solution.py:44
  297.4 12.2 %convolution_multiply_fusion.2 = f32[64,128,512]{2,1,0:T(8,128)} fusion(f32[64]{0:T(128)S(1)} %dynamic_slice.39, bf16[64,128,512]{2,1,0:T(8,128)(2,1)} %gather_fusion, pred[64]{0:T(512)(128)(4,1)S(1)} %get-tuple-element.114, bf16[256,128,128]{2,1,0:T(8,128)(2,1)} %get-tuple-element.141, s32[]{:T(128)S(6)} %select_n.70), kind=kOutput, calls=%fused_computation.4.clone.1 | convolution fusion | flops 1082130432 | bytes 27263300 | tf_op jit(solution)/shard_map/while/body/eval_jaxpr/kab,kbw->kaw/dot_general | solution.py:45
  309.5 36.7 %scatter_fusion = f32[32,128,512]{2,1,0:T(8,128)} fusion(f32[32,128,512]{2,1,0:T(8,128)} %get-tuple-element.127, s32[64]{0:T(128)S(1)} %fusion.19, f32[64,128,512]{2,1,0:T(8,128)} %convolution_multiply_fusion.2), kind=kCustom, calls=%fused_computation.3.clone.1 | custom fusion | flops 4194304 | bytes 50331904 | tf_op jit(solution)/shard_map/while/body/eval_jaxpr/scatter-add | solution.py:46
  347.8 7.9 %gather_fusion = bf16[64,128,512]{2,1,0:T(8,128)(2,1)} fusion(bf16[36,128,512]{2,1,0:T(8,128)(2,1)} %get-tuple-element.142, s32[1024]{0:T(1024)S(1)} %pad_clamp_fusion.4), kind=kCustom, calls=%fused_computation.1.clone.1 | custom fusion | bytes 16777472 | tf_op jit(solution)/shard_map/while/body/eval_jaxpr/jit(_take)/gather | solution.py:44
  355.7 12.2 %convolution_multiply_fusion.2 = f32[64,128,512]{2,1,0:T(8,128)} fusion(f32[64]{0:T(128)S(1)} %dynamic_slice.39, bf16[64,128,512]{2,1,0:T(8,128)(2,1)} %gather_fusion, pred[64]{0:T(512)(128)(4,1)S(1)} %get-tuple-element.114, bf16[256,128,128]{2,1,0:T(8,128)(2,1)} %get-tuple-element.141, s32[]{:T(128)S(6)} %select_n.70), kind=kOutput, calls=%fused_computation.4.clone.1 | convolution fusion | flops 1082130432 | bytes 27263300 | tf_op jit(solution)/shard_map/while/body/eval_jaxpr/kab,kbw->kaw/dot_general | solution.py:45
  367.8 36.4 %scatter_fusion = f32[32,128,512]{2,1,0:T(8,128)} fusion(f32[32,128,512]{2,1,0:T(8,128)} %get-tuple-element.127, s32[64]{0:T(128)S(1)} %fusion.19, f32[64,128,512]{2,1,0:T(8,128)} %convolution_multiply_fusion.2), kind=kCustom, calls=%fused_computation.3.clone.1 | custom fusion | flops 4194304 | bytes 50331904 | tf_op jit(solution)/shard_map/while/body/eval_jaxpr/scatter-add | solution.py:46
  405.9 7.9 %gather_fusion = bf16[64,128,512]{2,1,0:T(8,128)(2,1)} fusion(bf16[36,128,512]{2,1,0:T(8,128)(2,1)} %get-tuple-element.142, s32[1024]{0:T(1024)S(1)} %pad_clamp_fusion.4), kind=kCustom, calls=%fused_computation.1.clone.1 | custom fusion | bytes 16777472 | tf_op jit(solution)/shard_map/while/body/eval_jaxpr/jit(_take)/gather | solution.py:44
  413.7 12.2 %convolution_multiply_fusion.2 = f32[64,128,512]{2,1,0:T(8,128)} fusion(f32[64]{0:T(128)S(1)} %dynamic_slice.39, bf16[64,128,512]{2,1,0:T(8,128)(2,1)} %gather_fusion, pred[64]{0:T(512)(128)(4,1)S(1)} %get-tuple-element.114, bf16[256,128,128]{2,1,0:T(8,128)(2,1)} %get-tuple-element.141, s32[]{:T(128)S(6)} %select_n.70), kind=kOutput, calls=%fused_computation.4.clone.1 | convolution fusion | flops 1082130432 | bytes 27263300 | tf_op jit(solution)/shard_map/while/body/eval_jaxpr/kab,kbw->kaw/dot_general | solution.py:45
  425.9 36.4 %scatter_fusion = f32[32,128,512]{2,1,0:T(8,128)} fusion(f32[32,128,512]{2,1,0:T(8,128)} %get-tuple-element.127, s32[64]{0:T(128)S(1)} %fusion.19, f32[64,128,512]{2,1,0:T(8,128)} %convolution_multiply_fusion.2), kind=kCustom, calls=%fused_computation.3.clone.1 | custom fusion | flops 4194304 | bytes 50331904 | tf_op jit(solution)/shard_map/while/body/eval_jaxpr/scatter-add | solution.py:46
  462.3 4.2 convert_element_type.10
  466.9 3.4 fusion.9
  470.3 270.7 %all-reduce.5.cloned.1.call-done = f32[512,512]{1,0:T(8,128)} async-done(((f32[512,512]{1,0:T(8,128)}), f32[512,512]{1,0:T(8,128)}) %all-reduce.5.cloned.1.call-update) | async-done | bytes 1048592 | tf_op jit(solution)/shard_map/psum | solution.py:63
  (48 shorter events, 7.6 us)
Async XLA Ops:
  6.5 2.3 copy-start.2
  6.5 195.0 %all-reduce.3.cloned.1.call-start = ((), (), s32[]{:S(2)}) async-start(), calls=%async_computation | async-start | bytes 8388608 | tf_op jit(solution)/shard_map/psum | solution.py:15
  8.8 732.1 %all-reduce.5.cloned.1.call-start = ((), (), s32[]{:S(2)}) async-start(), calls=%async_computation.1 | async-start | bytes 2097152 | tf_op jit(solution)/shard_map/psum | solution.py:63
  205.5 10.4 %collective-permute-start = (bf16[256,512]{1,0:T(8,128)(2,1)S(1)}, bf16[256,512]{1,0:T(8,128)(2,1)S(1)}, u32[]{:S(2)}, u32[]{:S(2)}) collective-permute-start(bf16[256,512]{1,0:T(8,128)(2,1)S(1)} %broadcast_select_fusion.2), channel_id=1, source_target_pairs={{0,8},{8,16},{16,24},{24,32},{32,40},{40,48},{48,56},{56,64},{64,7... | collective-permute-start | bytes 786440 | tf_op jit(solution)/shard_map/ppermute | solution.py:10
  213.3 7.7 %collective-permute-start.1 = (bf16[256,512]{1,0:T(8,128)(2,1)S(1)}, bf16[256,512]{1,0:T(8,128)(2,1)S(1)}, u32[]{:S(2)}, u32[]{:S(2)}) collective-permute-start(bf16[256,512]{1,0:T(8,128)(2,1)S(1)} %broadcast_select_fusion.1), channel_id=1, source_target_pairs={{8,0},{16,8},{24,16},{32,24},{40,32},{48,40},{56,48},{64,56},{72,6... | collective-permute-start | bytes 786440 | tf_op jit(solution)/shard_map/ppermute | solution.py:10
  215.9 13.4 %copy-start.1 = (s32[256,2]{0,1:T(2,128)S(1)}, s32[256,2]{0,1:T(2,128)}, u32[]{:S(2)}) copy-start(s32[256,2]{0,1:T(2,128)} %param.11) | copy-start | bytes 6148
  462.3 4.6 copy-start
Sparse Core Ops, SparseCore 0:
  10.0 191.4 all-reduce.2
  470.4 270.5 all-reduce.4
where the time goes:
time: 750 us; the launch traced here: 749 us
  waiting for transfers between devices  468 us (62%)
  other arithmetic  158 us (21%)
  matrix products  52 us (7%)
  local copies, waits for them, and re-layouts  48.4 us (6%)
  between operations  14.2 us (2%)
    psum x1, waiting for transfers between devices, body(): total = lax.psum(contract(interface_mass_panel, tmat), 'dom')  271 us
    psum x1, waiting for transfers between devices, broadcast(): return lax.psum(block, axis)  193 us
    scatter-add x4, other arithmetic, step(): acc = acc.at[targets].add(prod * weights[:, None, None])  146 us
    dot_general x4, matrix products, step(): jnp.einsum('kab,kbw->kaw', blocks, selected, preferred_element_type=jnp.f...  48.6 us
    gather x4, local copies, waits for them, and re-layouts, step(): selected = jnp.take(extended, columns, axis=0)  31.5 us
  transfers between devices with their start and end apart: 4, of which 3 were waited for; matrix products, arithmetic and copies ran while one was open for 1% of the time, Pallas kernels for 0%

commit v1 on v0

--- a/solution.py
+++ b/solution.py
@@ -12,7 +12,12 @@
 
 def broadcast(block, axis, holder):
     block = jnp.where(lax.axis_index(axis) == holder, block, jnp.zeros_like(block))
-    return lax.psum(block, axis)
+
+    def supply_trees(values):
+        view_out = jnp.sum(lax.all_gather(values, axis_name=axis), axis=0)
+        return view_out
+
+    return supply_trees(block)
 
 
 def contract(left, right):

time: 750 us -> 1220 us (1.63)
  waiting for transfers between devices: 468 us -> 923 us
  other arithmetic: 158 us -> 172 us
    all_gather x0 -> x1, waiting for transfers between devices: none -> 648 us  [supply_trees(): view_out = jnp.sum(lax.all_gather(values, axis_name=axis), axis=0)]
    psum x1 -> x0, waiting for transfers between devices: 193 us -> none  [broadcast(): return lax.psum(block, axis)]
    reduce_sum x0 -> x1, other arithmetic: none -> 14.1 us  [supply_trees(): view_out = jnp.sum(lax.all_gather(values, axis_name=axis), axis=0)]
  transfers between devices with their start and end apart: 4 -> 4, of which waited for: 3 -> 4; matrix products, arithmetic and copies ran while one was open for 1% -> 0% of each run, Pallas kernels for 0% -> 0%
where the time goes in v1:
time: 1220 us
  waiting for transfers between devices  923 us (76%)
  other arithmetic  172 us (14%)
  matrix products  52.1 us (4%)
  local copies, waits for them, and re-layouts  48.8 us (4%)
  between operations  14.2 us (1%)
    all_gather x1, waiting for transfers between devices, supply_trees(): view_out = jnp.sum(lax.all_gather(values, axis_name=axis), axis=0)  648 us
    psum x1, waiting for transfers between devices, body(): total = lax.psum(contract(interface_mass_panel, tmat), 'dom')  270 us
    scatter-add x4, other arithmetic, step(): acc = acc.at[targets].add(prod * weights[:, None, None])  146 us
    dot_general x4, matrix products, step(): jnp.einsum('kab,kbw->kaw', blocks, selected, preferred_element_type=jnp.f...  48.7 us
    gather x4, local copies, waits for them, and re-layouts, step(): selected = jnp.take(extended, columns, axis=0)  31.9 us
  transfers between devices with their start and end apart: 4, of which 4 were waited for; matrix products, arithmetic and copies ran while one was open for 0% of the time, Pallas kernels for 0%

profile of v1, /device:TPU:1, one launch (start us, length us, event | category | flops | bytes accessed | tf_op | source)
XLA Modules:
  0.0 1218.2 jit_solution(2729107689817956845)
XLA Ops:
  8.9 648.4 %all-gather.3.cloned.1.call-done = bf16[32768,512]{1,0:T(8,128)(2,1)} async-done(((bf16[4096,512]{1,0:T(8,128)(2,1)}), bf16[32768,512]{1,0:T(8,128)(2,1)}) %all-gather.3.cloned.1.call-update) | async-done | bytes 33554448 | tf_op jit(solution)/shard_map/all_gather | solution.py:17
  657.3 14.1 %reduce_sum.12 = bf16[4096,512]{1,0:T(8,128)(2,1)} reduce(bf16[8,4096,512]{2,1,0:T(8,128)(2,1)} %bitcast.24, bf16[]{:T(256)} %constant.59.clone.1), dimensions={0}, to_apply=%region_0.1 | reduce | flops 14680064 | bytes 37748736 | tf_op jit(solution)/shard_map/reduce_sum | solution.py:17
  671.4 3.9 gather_fusion.2
  675.3 3.9 gather_fusion.1
  679.4 3.7 collective-permute-start
  686.4 4.5 collective-permute-done.1
  690.9 3.9 pad_maximum_fusion
  694.8 4.3 broadcast_in_dim.27
  699.1 233.3 %while.10 = (s32[]{:T(128)}, f32[32,128,512]{2,1,0:T(8,128)}, s32[256,2]{0,1:T(2,128)S(1)}, s32[4]{0:T(128)S(1)}, bf16[256,128,128]{2,1,0:T(8,128)(2,1)}, /*inde...) while((s32[]{:T(128)}, f32[32,128,512]{2,1,0:T(8,128)}, ...), condition=%wide.region_3.5_spmd, body=%wide.region_1.0_spmd.sunk | while | flops 1086326400 | bytes 94382912 | solution.py:55
  700.7 8.0 gather_fusion
  708.7 12.2 %convolution_multiply_fusion.2 = f32[64,128,512]{2,1,0:T(8,128)} fusion(f32[64]{0:T(128)S(1)} %dynamic_slice.39, bf16[64,128,512]{2,1,0:T(8,128)(2,1)} %gather_fusion, pred[64]{0:T(512)(128)(4,1)S(1)} %get-tuple-element.114, bf16[256,128,128]{2,1,0:T(8,128)(2,1)} %get-tuple-element.141, s32[]{:T(128)S(6)} %select_n.70), kind=kOutput, calls=%fused_computation.4.clone.1 | convolution fusion | flops 1082130432 | bytes 27263300 | tf_op jit(solution)/shard_map/while/body/eval_jaxpr/kab,kbw->kaw/dot_general | solution.py:50
  720.9 37.0 %scatter_fusion = f32[32,128,512]{2,1,0:T(8,128)} fusion(f32[32,128,512]{2,1,0:T(8,128)} %get-tuple-element.127, s32[64]{0:T(128)S(1)} %fusion.19, f32[64,128,512]{2,1,0:T(8,128)} %convolution_multiply_fusion.2), kind=kCustom, calls=%fused_computation.3.clone.1 | custom fusion | flops 4194304 | bytes 50331904 | tf_op jit(solution)/shard_map/while/body/eval_jaxpr/scatter-add | solution.py:51
  759.5 8.0 gather_fusion
  767.4 12.2 %convolution_multiply_fusion.2 = f32[64,128,512]{2,1,0:T(8,128)} fusion(f32[64]{0:T(128)S(1)} %dynamic_slice.39, bf16[64,128,512]{2,1,0:T(8,128)(2,1)} %gather_fusion, pred[64]{0:T(512)(128)(4,1)S(1)} %get-tuple-element.114, bf16[256,128,128]{2,1,0:T(8,128)(2,1)} %get-tuple-element.141, s32[]{:T(128)S(6)} %select_n.70), kind=kOutput, calls=%fused_computation.4.clone.1 | convolution fusion | flops 1082130432 | bytes 27263300 | tf_op jit(solution)/shard_map/while/body/eval_jaxpr/kab,kbw->kaw/dot_general | solution.py:50
  779.6 36.5 %scatter_fusion = f32[32,128,512]{2,1,0:T(8,128)} fusion(f32[32,128,512]{2,1,0:T(8,128)} %get-tuple-element.127, s32[64]{0:T(128)S(1)} %fusion.19, f32[64,128,512]{2,1,0:T(8,128)} %convolution_multiply_fusion.2), kind=kCustom, calls=%fused_computation.3.clone.1 | custom fusion | flops 4194304 | bytes 50331904 | tf_op jit(solution)/shard_map/while/body/eval_jaxpr/scatter-add | solution.py:51
  817.7 8.0 gather_fusion
  825.7 12.2 %convolution_multiply_fusion.2 = f32[64,128,512]{2,1,0:T(8,128)} fusion(f32[64]{0:T(128)S(1)} %dynamic_slice.39, bf16[64,128,512]{2,1,0:T(8,128)(2,1)} %gather_fusion, pred[64]{0:T(512)(128)(4,1)S(1)} %get-tuple-element.114, bf16[256,128,128]{2,1,0:T(8,128)(2,1)} %get-tuple-element.141, s32[]{:T(128)S(6)} %select_n.70), kind=kOutput, calls=%fused_computation.4.clone.1 | convolution fusion | flops 1082130432 | bytes 27263300 | tf_op jit(solution)/shard_map/while/body/eval_jaxpr/kab,kbw->kaw/dot_general | solution.py:50
  837.9 36.4 %scatter_fusion = f32[32,128,512]{2,1,0:T(8,128)} fusion(f32[32,128,512]{2,1,0:T(8,128)} %get-tuple-element.127, s32[64]{0:T(128)S(1)} %fusion.19, f32[64,128,512]{2,1,0:T(8,128)} %convolution_multiply_fusion.2), kind=kCustom, calls=%fused_computation.3.clone.1 | custom fusion | flops 4194304 | bytes 50331904 | tf_op jit(solution)/shard_map/while/body/eval_jaxpr/scatter-add | solution.py:51
  875.9 8.0 gather_fusion
  883.9 12.2 %convolution_multiply_fusion.2 = f32[64,128,512]{2,1,0:T(8,128)} fusion(f32[64]{0:T(128)S(1)} %dynamic_slice.39, bf16[64,128,512]{2,1,0:T(8,128)(2,1)} %gather_fusion, pred[64]{0:T(512)(128)(4,1)S(1)} %get-tuple-element.114, bf16[256,128,128]{2,1,0:T(8,128)(2,1)} %get-tuple-element.141, s32[]{:T(128)S(6)} %select_n.70), kind=kOutput, calls=%fused_computation.4.clone.1 | convolution fusion | flops 1082130432 | bytes 27263300 | tf_op jit(solution)/shard_map/while/body/eval_jaxpr/kab,kbw->kaw/dot_general | solution.py:50
  896.1 36.4 %scatter_fusion = f32[32,128,512]{2,1,0:T(8,128)} fusion(f32[32,128,512]{2,1,0:T(8,128)} %get-tuple-element.127, s32[64]{0:T(128)S(1)} %fusion.19, f32[64,128,512]{2,1,0:T(8,128)} %convolution_multiply_fusion.2), kind=kCustom, calls=%fused_computation.3.clone.1 | custom fusion | flops 4194304 | bytes 50331904 | tf_op jit(solution)/shard_map/while/body/eval_jaxpr/scatter-add | solution.py:51
  932.5 4.2 convert_element_type.12
  937.0 3.4 fusion.9
  940.4 269.5 %all-reduce.2.cloned.1.call-done = f32[512,512]{1,0:T(8,128)} async-done(((f32[512,512]{1,0:T(8,128)}), f32[512,512]{1,0:T(8,128)}) %all-reduce.2.cloned.1.call-update) | async-done | bytes 1048592 | tf_op jit(solution)/shard_map/psum | solution.py:68
  (49 shorter events, 10.4 us)
Async XLA Ops:
  6.5 2.3 copy-start.2
  6.5 650.8 %all-gather.3.cloned.1.call-start = ((), (), s32[]{:S(2)}) async-start(), calls=%async_computation.1 | async-start | bytes 37748736 | tf_op jit(solution)/shard_map/all_gather | solution.py:17
  8.8 1201.2 %all-reduce.2.cloned.1.call-start = ((), (), s32[]{:S(2)}) async-start(), calls=%async_computation | async-start | bytes 2097152 | tf_op jit(solution)/shard_map/psum | solution.py:68
  679.4 7.0 collective-permute-start
  683.2 7.7 collective-permute-start.1
  686.0 13.1 %copy-start.1 = (s32[256,2]{0,1:T(2,128)S(1)}, s32[256,2]{0,1:T(2,128)}, u32[]{:S(2)}) copy-start(s32[256,2]{0,1:T(2,128)} %param.11) | copy-start | bytes 6148
  932.5 4.6 copy-start
Sparse Core Ops, SparseCore 0:
  9.1 648.1 all-gather.2
  940.6 269.3 all-reduce.1
